TPU v7x, 256 devices: a whole 4x4x8 slice. The times are simulated.
256 devices in a mesh: row: 16 (over z, y_hi), col: 16 (over y_lo, x, core).
Axes of the slice: x: 4, y: 4 (y_hi: 2, y_lo: 2; y = y_hi * 2 + y_lo), z: 8, core: 2. Of those that a mesh axis runs over, the one named last changes fastest.
Arguments:
- object_field: float32 [2, 4096, 4096], P(None, 'row', 'col'), may hold values from -5 to 5
- probe: float32 [2, 256, 256], replicated, may hold values from -6 to 6
- amplitudes: float32 [16, 16, 4, 256, 256], P('row', 'col'), may hold values from 0 to 11, as said below
- positions: int32 [16, 16, 4, 2], P('row', 'col'), may hold values from 0 to 64
Outputs:
- object_next: float32 [2, 4096, 4096], P(None, 'row', 'col')
- probe_next: float32 [2, 256, 256], replicated
Inputs may be any that keep to these rules, and one draw needn't show every extreme that they name: Positive amplitudes.
All inputs are finite; a program needn't handle non-finite values.
Results may differ from a plain program's by a relative error of at most 0.0003.
Values sent between devices are 32-bit elements; how exact they have to be, the bound alone decides.
A program may use at most 64 MiB of HBM per device.

v0:
```python
import math
import jax
import jax.numpy as jnp
from jax import lax
from jax.sharding import PartitionSpec as P

W = 256
MARGIN = 32
smoothing = 0.1
regular = 1.0
epsilon = 1e-06


def padded(block, sides, width):
    for axis, dim in sides:
        count = lax.axis_size(axis)
        forward = [(i, i + 1) for i in range(count - 1)]
        backward = [(target, source) for source, target in forward]
        low = lax.ppermute(
            lax.slice_in_dim(block, block.shape[dim] - width, None, axis=dim), axis, forward
        )
        high = lax.ppermute(lax.slice_in_dim(block, 0, width, axis=dim), axis, backward)
        block = jnp.concatenate([low, block, high], axis=dim)
    return block


def shifted(block, axis, distance):
    devices = range(lax.axis_size(axis))
    route = [(i - distance, i) for i in devices if i - distance in devices]
    return lax.ppermute(block, axis, route)


def tables(length):
    indices = jnp.arange(length, dtype=jnp.int32)
    phases = (indices[:, None] * indices[None, :] % length).astype(jnp.float32) * (
        2.0 * math.pi / length
    )
    scaling = 1.0 / math.sqrt(length)
    cosine = jnp.cos(phases) * scaling
    sines = jnp.sin(phases) * scaling
    forward = jnp.concatenate(
        [jnp.concatenate([cosine, sines], 1), jnp.concatenate([-sines, cosine], 1)], 0
    )
    inverse = jnp.concatenate(
        [jnp.concatenate([cosine, -sines], 1), jnp.concatenate([sines, cosine], 1)], 0
    )
    return (forward, inverse)


def transform(wavefield, left_matrix, right_matrix):
    length = wavefield.shape[1]
    stacked = wavefield.reshape(2 * length, length)
    mixed = jnp.dot(left_matrix, stacked, precision=lax.Precision.HIGHEST)
    paired = jnp.concatenate([mixed[:length], mixed[length:]], axis=1)
    result = jnp.dot(paired, right_matrix, precision=lax.Precision.HIGHEST)
    return jnp.stack([result[:, :length], result[:, length:]])


def frame_terms(probe, window, amplitude, forward, inverse):
    exit_real = probe[0] * window[0] - probe[1] * window[1]
    exit_imag = probe[0] * window[1] + probe[1] * window[0]
    wave = jnp.stack([exit_real, exit_imag])
    far_field = transform(wave, forward, inverse)
    factor = amplitude / jnp.sqrt(
        far_field[0] * far_field[0] + far_field[1] * far_field[1] + smoothing
    )
    near_field = transform(far_field * factor[None], inverse, forward)
    difference = near_field - wave
    object_real = probe[0] * difference[0] + probe[1] * difference[1]
    object_imag = probe[0] * difference[1] - probe[1] * difference[0]
    probe_real = window[0] * difference[0] + window[1] * difference[1]
    probe_imag = window[0] * difference[1] - window[1] * difference[0]
    window_power = window[0] * window[0] + window[1] * window[1]
    return (
        jnp.stack([object_real, object_imag]),
        jnp.stack([probe_real, probe_imag, window_power]),
    )


def add_edges(middle, leading, trailing, along, tile_side, margin):
    head_pad = [(0, 0), (0, 0), (0, 0)]
    tail_pad = [(0, 0), (0, 0), (0, 0)]
    head_pad[along] = (0, tile_side - margin)
    tail_pad[along] = (tile_side - margin, 0)
    return middle + jnp.pad(leading, head_pad) + jnp.pad(trailing, tail_pad)


def per_device(object_field, probe, amplitudes, positions):
    forward, inverse = tables(W)
    tile_side = object_field.shape[1]
    margin = MARGIN
    window_side = tile_side + 2 * margin
    extended = padded(object_field, (("row", 1), ("col", 2)), MARGIN)
    power_map = probe[0] * probe[0] + probe[1] * probe[1]
    measured = amplitudes[0, 0]
    offsets = positions[0, 0]
    frame_total = measured.shape[0]
    anchor = jnp.zeros((), jnp.int32)

    def visit(frame_index, carried):
        canvas, probe_acc = carried
        amplitude = measured[frame_index]
        offset = offsets[frame_index]
        window = lax.dynamic_slice(extended, (anchor, offset[0], offset[1]), (2, W, W))
        object_term, probe_term = frame_terms(probe, window, amplitude, forward, inverse)
        update = jnp.concatenate([object_term, power_map[None]], 0)
        current = lax.dynamic_slice(canvas, (anchor, offset[0], offset[1]), (3, W, W))
        canvas = lax.dynamic_update_slice(canvas, current + update, (anchor, offset[0], offset[1]))
        return (canvas, probe_acc + probe_term)

    canvas_start = jnp.zeros((3, window_side, window_side), jnp.float32)
    probe_start = jnp.zeros((3, W, W), jnp.float32)
    canvas, probe_acc = lax.fori_loop(0, frame_total, visit, (canvas_start, probe_start))
    from_above = shifted(canvas[:, window_side - margin :, :], "row", 1)
    from_below = shifted(canvas[:, :margin, :], "row", -1)
    row_folded = add_edges(
        canvas[:, margin : margin + tile_side, :], from_above, from_below, 1, tile_side, margin
    )
    from_before = shifted(row_folded[:, :, window_side - margin :], "col", 1)
    from_after = shifted(row_folded[:, :, :margin], "col", -1)
    folded = add_edges(
        row_folded[:, :, margin : margin + tile_side], from_before, from_after, 2, tile_side, margin
    )
    object_next = object_field + folded[0:2] / (folded[2] + regular)
    local_target = jnp.sum(measured * measured)
    devices = lax.axis_size("row") * lax.axis_size("col")
    frame_count = frame_total * devices
    totals, target_sum = lax.psum((probe_acc, local_target), ("row", "col"))
    stepped = probe + totals[0:2] / (totals[2] + regular)
    probe_power = jnp.sum(stepped * stepped)
    target = target_sum / frame_count
    probe_next = stepped * jnp.sqrt(target / (probe_power + epsilon))
    return (object_next, probe_next)


def solution(mesh):
    return jax.shard_map(
        per_device,
        mesh=mesh,
        in_specs=(
            P(None, "row", "col"),
            P(),
            P("row", "col", None, None, None),
            P("row", "col", None, None),
        ),
        out_specs=(P(None, "row", "col"), P()),
        check_vma=False,
    )
```

profile of v0, /device:TPU:2, one launch (start us, length us, event | category | flops | bytes accessed | tf_op | source)
XLA Modules:
  0.0 516.5 jit_solution(1246306254406606753)
XLA Ops:
  8.2 5.1 collective-permute-start
  18.5 2.5 collective-permute-done.1
  21.9 1.9 collective-permute-start.2
  23.8 3.6 collective-permute-start.3
  27.7 2.9 collective-permute-done.2
  32.3 2.4 pad_maximum_fusion.5
  36.0 107.6 %while.16 = (s32[]{:T(128)}, f32[3,320,320]{2,1,0:T(8,128)}, f32[3,256,256]{2,1,0:T(8,128)}, s32[4,2]{0,1:T(2,128)S(1)}, f32[2,256,256]{2,1,0:T(8,128)S(1)}, /*i...) while((s32[]{:T(128)}, f32[3,320,320]{2,1,0:T(8,128)}, ...), condition=%wide.region_1.2_spmd.clone, body=%wide.region_0.1_spmd.clone.sunk | while | flops 3225354240 | bytes 31064388 | solution.py:113
  41.9 1.9 convolution_bitcast_fusion.4
  45.9 1.9 convolution_bitcast_fusion.5
  51.4 2.9 maximum_add_fusion.3
  54.3 8.7 %dynamic_update_slice.9 = f32[3,320,320]{2,1,0:T(8,128)} dynamic-update-slice(f32[3,320,320]{2,1,0:T(8,128)} %get-tuple-element.377, f32[3,256,256]{2,1,0:T(8,128)S(1)} %get-tuple-element.360, s32[]{:T(128)} %constant.57.clone.1..sunk, s32[]{:T(128)S(6)} %select_n.61, s32[]{:T(128)S(6)} %select_n.62) | dynamic-update-slice | bytes 1572868 | tf_op jit(solution)/shard_map/while/body/eval_jaxpr/dynamic_update_slice | solution.py:108
  73.0 1.9 convolution_bitcast_fusion.5
  78.5 3.2 maximum_add_fusion.3
  81.7 8.5 %dynamic_update_slice.9 = f32[3,320,320]{2,1,0:T(8,128)} dynamic-update-slice(f32[3,320,320]{2,1,0:T(8,128)} %get-tuple-element.377, f32[3,256,256]{2,1,0:T(8,128)S(1)} %get-tuple-element.360, s32[]{:T(128)} %constant.57.clone.1..sunk, s32[]{:T(128)S(6)} %select_n.61, s32[]{:T(128)S(6)} %select_n.62) | dynamic-update-slice | bytes 1572868 | tf_op jit(solution)/shard_map/while/body/eval_jaxpr/dynamic_update_slice | solution.py:108
  105.6 3.2 maximum_add_fusion.3
  108.8 8.5 %dynamic_update_slice.9 = f32[3,320,320]{2,1,0:T(8,128)} dynamic-update-slice(f32[3,320,320]{2,1,0:T(8,128)} %get-tuple-element.377, f32[3,256,256]{2,1,0:T(8,128)S(1)} %get-tuple-element.360, s32[]{:T(128)} %constant.57.clone.1..sunk, s32[]{:T(128)S(6)} %select_n.61, s32[]{:T(128)S(6)} %select_n.62) | dynamic-update-slice | bytes 1572868 | tf_op jit(solution)/shard_map/while/body/eval_jaxpr/dynamic_update_slice | solution.py:108
  132.7 3.2 maximum_add_fusion.3
  135.9 7.6 %dynamic_update_slice.9 = f32[3,320,320]{2,1,0:T(8,128)} dynamic-update-slice(f32[3,320,320]{2,1,0:T(8,128)} %get-tuple-element.377, f32[3,256,256]{2,1,0:T(8,128)S(1)} %get-tuple-element.360, s32[]{:T(128)} %constant.57.clone.1..sunk, s32[]{:T(128)S(6)} %select_n.61, s32[]{:T(128)S(6)} %select_n.62) | dynamic-update-slice | bytes 1572868 | tf_op jit(solution)/shard_map/while/body/eval_jaxpr/dynamic_update_slice | solution.py:108
  144.5 5.3 %collective-permute-start.4 = (f32[3,32,320]{2,1,0:T(8,128)S(1)}, f32[3,32,320]{2,1,0:T(8,128)S(1)}, u32[]{:S(2)}, u32[]{:S(2)}) collective-permute-start(f32[3,32,320]{2,1,0:T(8,128)S(1)} %get-tuple-element.249), channel_id=1, source_target_pairs={{0,16},{16,32},{32,48},{48,64},{64,80},{80,96},{96,112},{112,128},... | collective-permute-start | bytes 368648 | tf_op jit(solution)/shard_map/ppermute | solution.py:30
  152.9 6.3 %collective-permute-done.5 = f32[3,32,320]{2,1,0:T(8,128)S(1)} collective-permute-done((f32[3,32,320]{2,1,0:T(8,128)S(1)}, f32[3,32,320]{2,1,0:T(8,128)S(1)}, u32[]{:S(2)}, u32[]{:S(2)}) %collective-permute-start.5) | collective-permute-done | bytes 122912 | tf_op jit(solution)/shard_map/ppermute | solution.py:30
  160.8 2.6 collective-permute-start.6
  163.4 3.0 collective-permute-start.7
  167.3 81.6 %psum.15 = f32[]{:T(128)} all-reduce(f32[]{:T(128)} %multiply_reduce_fusion), channel_id=1, replica_groups=mesh['row'=16,'col'=16] {'row','col'}, use_global_device_ids=true, to_apply=%region_4.5 | all-reduce | flops 1 | bytes 8 | tf_op jit(solution)/shard_map/psum | solution.py:128
  251.4 253.7 %all-reduce.6.cloned.1.call-done = f32[3,256,256]{2,1,0:T(8,128)} async-done(((f32[3,256,256]{2,1,0:T(8,128)}), f32[3,256,256]{2,1,0:T(8,128)}) %all-reduce.6.cloned.1.call-update) | async-done | bytes 786448 | tf_op jit(solution)/shard_map/psum | solution.py:128
  (107 shorter events, 62.5 us)
Async XLA Ops:
  7.2 11.3 %copy-start.3 = (f32[2,256,256]{2,1,0:T(8,128)S(1)}, f32[2,256,256]{2,1,0:T(8,128)}, u32[]{:S(2)}) copy-start(f32[2,256,256]{2,1,0:T(8,128)} %param.6) | copy-start | bytes 1572868
  7.2 498.0 %all-reduce.6.cloned.1.call-start = ((), (), s32[]{:S(2)}) async-start(), calls=%async_computation | async-start | bytes 1572864 | tf_op jit(solution)/shard_map/psum | solution.py:128
  8.2 10.2 %collective-permute-start = (f32[2,32,256]{2,1,0:T(8,128)S(1)}, f32[2,32,256]{2,1,0:T(8,128)S(1)}, u32[]{:S(2)}, u32[]{:S(2)}) collective-permute-start(f32[2,32,256]{2,1,0:T(8,128)S(1)} %get-tuple-element.258), channel_id=1, source_target_pairs={{0,16},{16,32},{32,48},{48,64},{64,80},{80,96},{96,112},{112,128},... | collective-permute-start | bytes 196616 | tf_op jit(solution)/shard_map/ppermute | solution.py:19
  13.3 7.7 %collective-permute-start.1 = (f32[2,32,256]{2,1,0:T(8,128)S(1)}, f32[2,32,256]{2,1,0:T(8,128)S(1)}, u32[]{:S(2)}, u32[]{:S(2)}) collective-permute-start(f32[2,32,256]{2,1,0:T(8,128)S(1)} %get-tuple-element.257), channel_id=1, source_target_pairs={{16,0},{32,16},{48,32},{64,48},{80,64},{96,80},{112,96},{128,112},... | collective-permute-start | bytes 196616 | tf_op jit(solution)/shard_map/ppermute | solution.py:22
  21.9 8.7 %collective-permute-start.2 = (f32[2,320,32]{2,1,0:T(8,128)}, f32[2,320,32]{2,1,0:T(8,128)}, u32[]{:S(2)}, u32[]{:S(2)}) collective-permute-start(f32[2,320,32]{2,1,0:T(8,128)} %get-tuple-element.255), channel_id=1, source_target_pairs={{0,1},{1,2},{2,3},{3,4},{4,5},{5,6},{6,7},{7,8},{8,9},{9,10},{10,1... | collective-permute-start | bytes 245768 | tf_op jit(solution)/shard_map/ppermute | solution.py:19
  23.8 8.5 %collective-permute-start.3 = (f32[2,320,32]{2,1,0:T(8,128)}, f32[2,320,32]{2,1,0:T(8,128)}, u32[]{:S(2)}, u32[]{:S(2)}) collective-permute-start(f32[2,320,32]{2,1,0:T(8,128)} %get-tuple-element.256), channel_id=1, source_target_pairs={{1,0},{2,1},{3,2},{4,3},{5,4},{6,5},{7,6},{8,7},{9,8},{10,9},{11,1... | collective-permute-start | bytes 245768 | tf_op jit(solution)/shard_map/ppermute | solution.py:22
  27.7 8.3 %copy-start = (f32[2,256,256]{2,1,0:T(8,128)S(1)}, f32[2,256,256]{2,1,0:T(8,128)}, u32[]{:S(2)}) copy-start(f32[2,256,256]{2,1,0:T(8,128)} %param.7) | copy-start | bytes 1572868
  27.7 8.3 %copy-start.6 = (s32[1,1,4,2]{2,3,1,0:T(2,128)S(1)}, s32[1,1,4,2]{2,3,1,0:T(2,128)}, u32[]{:S(2)}) copy-start(s32[1,1,4,2]{2,3,1,0:T(2,128)} %param.9) | copy-start | bytes 100
  48.9 1.2 copy-start.1
  76.0 1.2 copy-start.1
  103.1 1.2 copy-start.1
  130.2 1.2 copy-start.1
  144.5 8.4 %collective-permute-start.4 = (f32[3,32,320]{2,1,0:T(8,128)S(1)}, f32[3,32,320]{2,1,0:T(8,128)S(1)}, u32[]{:S(2)}, u32[]{:S(2)}) collective-permute-start(f32[3,32,320]{2,1,0:T(8,128)S(1)} %get-tuple-element.249), channel_id=1, source_target_pairs={{0,16},{16,32},{32,48},{48,64},{64,80},{80,96},{96,112},{112,128},... | collective-permute-start | bytes 368648 | tf_op jit(solution)/shard_map/ppermute | solution.py:30
  149.8 16.5 %copy-start.2 = (f32[4,256,256]{2,1,0:T(8,128)S(1)}, f32[4,256,256]{2,1,0:T(8,128)}, u32[]{:S(2)}) copy-start(f32[4,256,256]{2,1,0:T(8,128)} %get-tuple-element.408) | copy-start | bytes 3145732
  149.8 9.4 %collective-permute-start.5 = (f32[3,32,320]{2,1,0:T(8,128)S(1)}, f32[3,32,320]{2,1,0:T(8,128)S(1)}, u32[]{:S(2)}, u32[]{:S(2)}) collective-permute-start(f32[3,32,320]{2,1,0:T(8,128)S(1)} %get-tuple-element.250), channel_id=1, source_target_pairs={{16,0},{32,16},{48,32},{64,48},{80,64},{96,80},{112,96},{128,112},... | collective-permute-start | bytes 368648 | tf_op jit(solution)/shard_map/ppermute | solution.py:30
  160.8 88.7 %collective-permute-start.6 = (f32[3,256,32]{2,1,0:T(8,128)S(1)}, f32[3,256,32]{2,1,0:T(8,128)S(1)}, u32[]{:S(2)}, u32[]{:S(2)}) collective-permute-start(f32[3,256,32]{2,1,0:T(8,128)S(1)} %get-tuple-element.251), channel_id=1, source_target_pairs={{0,1},{1,2},{2,3},{3,4},{4,5},{5,6},{6,7},{7,8},{8,9},{9,10},{10,1... | collective-permute-start | bytes 294920 | tf_op jit(solution)/shard_map/ppermute | solution.py:30
  163.4 86.2 %collective-permute-start.7 = (f32[3,256,32]{2,1,0:T(8,128)S(1)}, f32[3,256,32]{2,1,0:T(8,128)S(1)}, u32[]{:S(2)}, u32[]{:S(2)}) collective-permute-start(f32[3,256,32]{2,1,0:T(8,128)S(1)} %get-tuple-element.252), channel_id=1, source_target_pairs={{1,0},{2,1},{3,2},{4,3},{5,4},{6,5},{7,6},{8,7},{9,8},{10,9},{11,1... | collective-permute-start | bytes 294920 | tf_op jit(solution)/shard_map/ppermute | solution.py:30
  249.5 1.0 copy-start.4
  505.2 3.6 copy-start.5
Sparse Core Ops, SparseCore 0:
  249.6 255.4 all-reduce.5
where the time goes:
time: 519 us; the launch traced here: 516 us
  waiting for transfers between devices  269 us (52%)
  blocking collectives  81.6 us (16%)
  local copies, waits for them, and re-layouts  45.4 us (9%)
  other arithmetic  41.4 us (8%)
  starting transfers between devices  24.3 us (5%)
  matrix products  23.4 us (5%)
  loops' own time  15.9 us (3%)
  between operations  15.6 us (3%)
    psum x1, waiting for transfers between devices, per_device(): totals, target_sum = lax.psum((probe_acc, local_target), ('row', 'col'))  254 us
    psum x1, blocking collectives, per_device(): totals, target_sum = lax.psum((probe_acc, local_target), ('row', 'col'))  81.6 us
    dynamic_update_slice x4, local copies, waits for them, and re-layouts, visit(): lax.dynamic_update_slice(canvas, current + update, (anchor, offset[0], of...  33.4 us
    another operation x1, loops' own time, per_device(): lax.fori_loop(0, frame_total, visit, (canvas_start, probe_start))  15.9 us
    dot_general x8, matrix products, transform(): mixed = jnp.dot(left_matrix, stacked, precision=lax.Precision.HIGHEST)  14.9 us
    add x4, other arithmetic, visit(): current + update  12.6 us
    ppermute x4, starting transfers between devices, shifted(): return lax.ppermute(block, axis, route)  12.3 us
  transfers between devices with their start and end apart: 9, of which 6 were waited for; matrix products, arithmetic and copies ran while one was open for 1% of the time, Pallas kernels for 0%

commit v1 on v0

--- a/solution.py
+++ b/solution.py
@@ -3,12 +3,19 @@
 import jax.numpy as jnp
 from jax import lax
 from jax.sharding import PartitionSpec as P
+from jax.lax import psum
 
 W = 256
 MARGIN = 32
 smoothing = 0.1
 regular = 1.0
 epsilon = 1e-06
+
+
+def meet_things(my_data):
+    for tick in ("row", "col"):
+        my_data = psum(my_data, axis_name=tick)
+    return my_data
 
 
 def padded(block, sides, width):
@@ -125,7 +132,7 @@
     local_target = jnp.sum(measured * measured)
     devices = lax.axis_size("row") * lax.axis_size("col")
     frame_count = frame_total * devices
-    totals, target_sum = lax.psum((probe_acc, local_target), ("row", "col"))
+    totals, target_sum = meet_things((probe_acc, local_target))
     stepped = probe + totals[0:2] / (totals[2] + regular)
     probe_power = jnp.sum(stepped * stepped)
     target = target_sum / frame_count

time: 519 us -> 453 us (0.87)
  waiting for transfers between devices: 269 us -> 213 us
  blocking collectives: 81.6 us -> 65.8 us
    psum x1 -> x2, waiting for transfers between devices: 254 us -> 198 us  [meet_things(): my_data = psum(my_data, axis_name=tick)]
    psum x1 -> x2, blocking collectives: 81.6 us -> 65.8 us  [meet_things(): my_data = psum(my_data, axis_name=tick)]
  transfers between devices with their start and end apart: 9 -> 10, of which waited for: 6 -> 7; matrix products, arithmetic and copies ran while one was open for 1% -> 2% of each run, Pallas kernels for 0% -> 0%
where the time goes in v1:
time: 453 us; the launch traced here: 447 us
  waiting for transfers between devices  213 us (47%)
  blocking collectives  65.8 us (15%)
  local copies, waits for them, and re-layouts  44.8 us (10%)
  other arithmetic  43.5 us (10%)
  starting transfers between devices  24.2 us (5%)
  matrix products  23.4 us (5%)
  loops' own time  15.9 us (4%)
  between operations  15.6 us (3%)
    psum x2, waiting for transfers between devices, meet_things(): my_data = psum(my_data, axis_name=tick)  198 us
    psum x2, blocking collectives, meet_things(): my_data = psum(my_data, axis_name=tick)  65.8 us
    dynamic_update_slice x4, local copies, waits for them, and re-layouts, visit(): lax.dynamic_update_slice(canvas, current + update, (anchor, offset[0], of...  33.4 us
    another operation x1, loops' own time, per_device(): lax.fori_loop(0, frame_total, visit, (canvas_start, probe_start))  15.9 us
    dot_general x8, matrix products, transform(): mixed = jnp.dot(left_matrix, stacked, precision=lax.Precision.HIGHEST)  14.9 us
    add x4, other arithmetic, visit(): current + update  12.5 us
    ppermute x4, starting transfers between devices, shifted(): return lax.ppermute(block, axis, route)  12.2 us
  transfers between devices with their start and end apart: 10, of which 7 were waited for; matrix products, arithmetic and copies ran while one was open for 2% of the time, Pallas kernels for 0%

profile of v1, /device:TPU:2, one launch (start us, length us, event | category | flops | bytes accessed | tf_op | source)
XLA Modules:
  0.0 446.6 jit_solution(11396383427636254170)
XLA Ops:
  8.2 5.1 %collective-permute-start = (f32[2,32,256]{2,1,0:T(8,128)S(1)}, f32[2,32,256]{2,1,0:T(8,128)S(1)}, u32[]{:S(2)}, u32[]{:S(2)}) collective-permute-start(f32[2,32,256]{2,1,0:T(8,128)S(1)} %get-tuple-element.258), channel_id=1, source_target_pairs={{0,16},{16,32},{32,48},{48,64},{64,80},{80,96},{96,112},{112,128},... | collective-permute-start | bytes 196616 | tf_op jit(solution)/shard_map/ppermute | solution.py:26
  18.4 2.5 collective-permute-done.1
  21.9 1.9 collective-permute-start.2
  23.8 3.6 collective-permute-start.3
  27.7 2.9 collective-permute-done.2
  32.3 2.4 pad_maximum_fusion.5
  36.0 107.5 %while.16 = (s32[]{:T(128)}, f32[3,320,320]{2,1,0:T(8,128)}, f32[3,256,256]{2,1,0:T(8,128)}, s32[4,2]{0,1:T(2,128)S(1)}, f32[2,256,256]{2,1,0:T(8,128)S(1)}, /*i...) while((s32[]{:T(128)}, f32[3,320,320]{2,1,0:T(8,128)}, ...), condition=%wide.region_1.2_spmd.clone, body=%wide.region_0.1_spmd.clone.sunk | while | flops 3225354240 | bytes 31064388 | solution.py:120
  51.4 2.9 maximum_add_fusion.3
  54.3 8.8 %dynamic_update_slice.9 = f32[3,320,320]{2,1,0:T(8,128)} dynamic-update-slice(f32[3,320,320]{2,1,0:T(8,128)} %get-tuple-element.377, f32[3,256,256]{2,1,0:T(8,128)S(1)} %get-tuple-element.360, s32[]{:T(128)} %constant.57.clone.1..sunk, s32[]{:T(128)S(6)} %select_n.61, s32[]{:T(128)S(6)} %select_n.62) | dynamic-update-slice | bytes 1572868 | tf_op jit(solution)/shard_map/while/body/eval_jaxpr/dynamic_update_slice | solution.py:115
  78.4 3.2 maximum_add_fusion.3
  81.6 8.5 %dynamic_update_slice.9 = f32[3,320,320]{2,1,0:T(8,128)} dynamic-update-slice(f32[3,320,320]{2,1,0:T(8,128)} %get-tuple-element.377, f32[3,256,256]{2,1,0:T(8,128)S(1)} %get-tuple-element.360, s32[]{:T(128)} %constant.57.clone.1..sunk, s32[]{:T(128)S(6)} %select_n.61, s32[]{:T(128)S(6)} %select_n.62) | dynamic-update-slice | bytes 1572868 | tf_op jit(solution)/shard_map/while/body/eval_jaxpr/dynamic_update_slice | solution.py:115
  105.5 3.2 maximum_add_fusion.3
  108.7 8.5 %dynamic_update_slice.9 = f32[3,320,320]{2,1,0:T(8,128)} dynamic-update-slice(f32[3,320,320]{2,1,0:T(8,128)} %get-tuple-element.377, f32[3,256,256]{2,1,0:T(8,128)S(1)} %get-tuple-element.360, s32[]{:T(128)} %constant.57.clone.1..sunk, s32[]{:T(128)S(6)} %select_n.61, s32[]{:T(128)S(6)} %select_n.62) | dynamic-update-slice | bytes 1572868 | tf_op jit(solution)/shard_map/while/body/eval_jaxpr/dynamic_update_slice | solution.py:115
  132.7 3.2 maximum_add_fusion.3
  135.8 7.6 %dynamic_update_slice.9 = f32[3,320,320]{2,1,0:T(8,128)} dynamic-update-slice(f32[3,320,320]{2,1,0:T(8,128)} %get-tuple-element.377, f32[3,256,256]{2,1,0:T(8,128)S(1)} %get-tuple-element.360, s32[]{:T(128)} %constant.57.clone.1..sunk, s32[]{:T(128)S(6)} %select_n.61, s32[]{:T(128)S(6)} %select_n.62) | dynamic-update-slice | bytes 1572868 | tf_op jit(solution)/shard_map/while/body/eval_jaxpr/dynamic_update_slice | solution.py:115
  144.5 5.3 %collective-permute-start.4 = (f32[3,32,320]{2,1,0:T(8,128)S(1)}, f32[3,32,320]{2,1,0:T(8,128)S(1)}, u32[]{:S(2)}, u32[]{:S(2)}) collective-permute-start(f32[3,32,320]{2,1,0:T(8,128)S(1)} %get-tuple-element.249), channel_id=1, source_target_pairs={{0,16},{16,32},{32,48},{48,64},{64,80},{80,96},{96,112},{112,128},... | collective-permute-start | bytes 368648 | tf_op jit(solution)/shard_map/ppermute | solution.py:37
  153.0 6.2 %collective-permute-done.5 = f32[3,32,320]{2,1,0:T(8,128)S(1)} collective-permute-done((f32[3,32,320]{2,1,0:T(8,128)S(1)}, f32[3,32,320]{2,1,0:T(8,128)S(1)}, u32[]{:S(2)}, u32[]{:S(2)}) %collective-permute-start.5) | collective-permute-done | bytes 122912 | tf_op jit(solution)/shard_map/ppermute | solution.py:37
  160.7 2.5 collective-permute-start.6
  163.3 3.0 collective-permute-start.7
  166.3 146.6 %all-reduce.7.cloned.1.call-done = f32[3,256,256]{2,1,0:T(8,128)} async-done(((f32[3,256,256]{2,1,0:T(8,128)}), f32[3,256,256]{2,1,0:T(8,128)}) %all-reduce.7.cloned.1.call-update) | async-done | bytes 786448 | tf_op jit(solution)/shard_map/psum | solution.py:17
  313.0 2.1 multiply_reduce_fusion
  315.1 41.8 %psum.30 = f32[]{:T(128)} all-reduce(f32[]{:T(128)} %multiply_reduce_fusion), channel_id=1, replica_groups=mesh['row'=16,'col'=16] {'row'}, use_global_device_ids=true, to_apply=%region_5.6 | all-reduce | flops 1 | bytes 8 | tf_op jit(solution)/shard_map/psum | solution.py:17
  356.9 23.9 %psum.31 = f32[]{:T(128)} all-reduce(f32[]{:T(128)} %psum.30), channel_id=1, replica_groups=mesh['row'=16,'col'=16] {'col'}, use_global_device_ids=true, to_apply=%region_6.7 | all-reduce | flops 1 | bytes 8 | tf_op jit(solution)/shard_map/psum | solution.py:17
  383.8 51.4 %all-reduce.9.cloned.1.call-done = f32[3,256,256]{2,1,0:T(8,128)} async-done(((f32[3,256,256]{2,1,0:T(8,128)}), f32[3,256,256]{2,1,0:T(8,128)}) %all-reduce.9.cloned.1.call-update) | async-done | bytes 786448 | tf_op jit(solution)/shard_map/psum | solution.py:17
  (109 shorter events, 67.6 us)
Async XLA Ops:
  7.2 11.2 %copy-start.2 = (f32[2,256,256]{2,1,0:T(8,128)S(1)}, f32[2,256,256]{2,1,0:T(8,128)}, u32[]{:S(2)}) copy-start(f32[2,256,256]{2,1,0:T(8,128)} %param.6) | copy-start | bytes 1572868
  7.2 305.8 %all-reduce.7.cloned.1.call-start = ((), (), s32[]{:S(2)}) async-start(), calls=%async_computation | async-start | bytes 1572864 | tf_op jit(solution)/shard_map/psum | solution.py:17
  8.2 10.2 %collective-permute-start = (f32[2,32,256]{2,1,0:T(8,128)S(1)}, f32[2,32,256]{2,1,0:T(8,128)S(1)}, u32[]{:S(2)}, u32[]{:S(2)}) collective-permute-start(f32[2,32,256]{2,1,0:T(8,128)S(1)} %get-tuple-element.258), channel_id=1, source_target_pairs={{0,16},{16,32},{32,48},{48,64},{64,80},{80,96},{96,112},{112,128},... | collective-permute-start | bytes 196616 | tf_op jit(solution)/shard_map/ppermute | solution.py:26
  13.3 7.7 %collective-permute-start.1 = (f32[2,32,256]{2,1,0:T(8,128)S(1)}, f32[2,32,256]{2,1,0:T(8,128)S(1)}, u32[]{:S(2)}, u32[]{:S(2)}) collective-permute-start(f32[2,32,256]{2,1,0:T(8,128)S(1)} %get-tuple-element.257), channel_id=1, source_target_pairs={{16,0},{32,16},{48,32},{64,48},{80,64},{96,80},{112,96},{128,112},... | collective-permute-start | bytes 196616 | tf_op jit(solution)/shard_map/ppermute | solution.py:29
  21.9 8.7 %collective-permute-start.2 = (f32[2,320,32]{2,1,0:T(8,128)}, f32[2,320,32]{2,1,0:T(8,128)}, u32[]{:S(2)}, u32[]{:S(2)}) collective-permute-start(f32[2,320,32]{2,1,0:T(8,128)} %get-tuple-element.255), channel_id=1, source_target_pairs={{0,1},{1,2},{2,3},{3,4},{4,5},{5,6},{6,7},{7,8},{8,9},{9,10},{10,1... | collective-permute-start | bytes 245768 | tf_op jit(solution)/shard_map/ppermute | solution.py:26
  23.8 8.5 %collective-permute-start.3 = (f32[2,320,32]{2,1,0:T(8,128)}, f32[2,320,32]{2,1,0:T(8,128)}, u32[]{:S(2)}, u32[]{:S(2)}) collective-permute-start(f32[2,320,32]{2,1,0:T(8,128)} %get-tuple-element.256), channel_id=1, source_target_pairs={{1,0},{2,1},{3,2},{4,3},{5,4},{6,5},{7,6},{8,7},{9,8},{10,9},{11,1... | collective-permute-start | bytes 245768 | tf_op jit(solution)/shard_map/ppermute | solution.py:29
  27.7 8.3 %copy-start = (f32[2,256,256]{2,1,0:T(8,128)S(1)}, f32[2,256,256]{2,1,0:T(8,128)}, u32[]{:S(2)}) copy-start(f32[2,256,256]{2,1,0:T(8,128)} %param.7) | copy-start | bytes 1572868
  27.7 8.3 %copy-start.5 = (s32[1,1,4,2]{2,3,1,0:T(2,128)S(1)}, s32[1,1,4,2]{2,3,1,0:T(2,128)}, u32[]{:S(2)}) copy-start(s32[1,1,4,2]{2,3,1,0:T(2,128)} %param.9) | copy-start | bytes 100
  48.9 1.2 copy-start.1
  76.0 1.2 copy-start.1
  103.1 1.2 copy-start.1
  130.2 1.2 copy-start.1
  143.5 291.8 %all-reduce.9.cloned.1.call-start = ((), (), s32[]{:S(2)}) async-start(), calls=%async_computation.1 | async-start | bytes 1572864 | tf_op jit(solution)/shard_map/psum | solution.py:17
  144.5 8.5 %collective-permute-start.4 = (f32[3,32,320]{2,1,0:T(8,128)S(1)}, f32[3,32,320]{2,1,0:T(8,128)S(1)}, u32[]{:S(2)}, u32[]{:S(2)}) collective-permute-start(f32[3,32,320]{2,1,0:T(8,128)S(1)} %get-tuple-element.249), channel_id=1, source_target_pairs={{0,16},{16,32},{32,48},{48,64},{64,80},{80,96},{96,112},{112,128},... | collective-permute-start | bytes 368648 | tf_op jit(solution)/shard_map/ppermute | solution.py:37
  149.9 9.3 %collective-permute-start.5 = (f32[3,32,320]{2,1,0:T(8,128)S(1)}, f32[3,32,320]{2,1,0:T(8,128)S(1)}, u32[]{:S(2)}, u32[]{:S(2)}) collective-permute-start(f32[3,32,320]{2,1,0:T(8,128)S(1)} %get-tuple-element.250), channel_id=1, source_target_pairs={{16,0},{32,16},{48,32},{64,48},{80,64},{96,80},{112,96},{128,112},... | collective-permute-start | bytes 368648 | tf_op jit(solution)/shard_map/ppermute | solution.py:37
  160.7 220.8 %collective-permute-start.6 = (f32[3,256,32]{2,1,0:T(8,128)S(1)}, f32[3,256,32]{2,1,0:T(8,128)S(1)}, u32[]{:S(2)}, u32[]{:S(2)}) collective-permute-start(f32[3,256,32]{2,1,0:T(8,128)S(1)} %get-tuple-element.251), channel_id=1, source_target_pairs={{0,1},{1,2},{2,3},{3,4},{4,5},{5,6},{6,7},{7,8},{8,9},{9,10},{10,1... | collective-permute-start | bytes 294920 | tf_op jit(solution)/shard_map/ppermute | solution.py:37
  163.3 218.3 %collective-permute-start.7 = (f32[3,256,32]{2,1,0:T(8,128)S(1)}, f32[3,256,32]{2,1,0:T(8,128)}, u32[]{:S(2)}, u32[]{:S(2)}) collective-permute-start(f32[3,256,32]{2,1,0:T(8,128)S(1)} %get-tuple-element.252), channel_id=1, source_target_pairs={{1,0},{2,1},{3,2},{4,3},{5,4},{6,5},{7,6},{8,7},{9,8},{10,9},{11,1... | collective-permute-start | bytes 294920 | tf_op jit(solution)/shard_map/ppermute | solution.py:37
  315.1 67.9 %copy-start.3 = (f32[2,256,256]{2,1,0:T(8,128)S(1)}, f32[2,256,256]{2,1,0:T(8,128)}, u32[]{:S(2)}) copy-start(f32[2,256,256]{2,1,0:T(8,128)} %param.6) | copy-start | bytes 1572868
  435.3 3.6 copy-start.4
Sparse Core Ops, SparseCore 0:
  143.6 169.3 all-reduce.6
  315.5 119.6 all-reduce.8
